TPU v7x, 512 devices: a whole 4x4x16 slice. The times are simulated.
512 devices in a mesh: leaf: 512 (over y, x, z, core).
Axes of the slice: x: 4, y: 4, z: 16, core: 2. Of those that a mesh axis runs over, the one named last changes fastest.
Arguments:
- vectors: float32 [512, 512, 128], P('leaf'), may hold values from -6 to 6
- points: float32 [512, 3, 512], P('leaf')
- leaf_basis: float32 [512, 512, 128], P('leaf'), may hold values from -0.25 to 0.25
- transfer_leaf: float32 [512, 128, 128], P('leaf'), may hold values from -0.5 to 0.5
- transfer_pair: float32 [32768, 128], P('leaf'), may hold values from -0.5 to 0.5
- transfer_quad: float32 [16384, 128], P('leaf'), may hold values from -0.5 to 0.5
- skel_leaf: float32 [512, 3, 128], P('leaf')
- skel_pair: float32 [256, 3, 128], replicated
- skel_quad: float32 [128, 3, 128], replicated
- skel_top: float32 [64, 3, 128], replicated
- near_list: int32 [512, 16], P('leaf'), may hold values from -1 to 511, as said below
- far_leaf: int32 [512, 8], P('leaf'), may hold values from -1 to 511, as said below
- far_pair: int32 [256, 8], replicated, may hold values from -1 to 255, as said below
- far_quad: int32 [128, 8], replicated, may hold values from -1 to 127, as said below
- far_top: int32 [64, 8], replicated, may hold values from -1 to 63, as said below
Outputs:
- product: float32 [512, 512, 128], P('leaf')
Inputs may be any that keep to these rules, and one draw needn't show every extreme that they name: `near_list`: entry 0 of row l is l; the other entries are distinct leaves within 8 of l, or -1 for an unused slot. `far_leaf`: distinct leaves within 8 of the row's leaf, none of them in that leaf's row of near_list, or -1 for an unused slot. `far_pair`: distinct clusters within 4 of the row's cluster and other than it, or -1 for an unused slot. `far_quad`: distinct clusters within 4 of the row's cluster and other than it, or -1 for an unused slot. `far_top`: distinct top clusters other than the row's cluster, or -1 for an unused slot.
All inputs are finite; a program needn't handle non-finite values.
Results may differ from a plain program's by a relative error of at most 0.0003.
Values sent between devices are 32-bit elements; how exact they have to be, the bound alone decides.
A program may use at most 64 MiB of HBM per device.

v0:
```python
import jax
import jax.numpy as jnp
from jax import lax
from jax.sharding import PartitionSpec as P

REACH = 8
FAR_REACH = 4
INV_FOUR_PI = 0.07957747154594767
DELTA_SQ = 0.01
HIGHEST = lax.Precision.HIGHEST


def from_partner(value, axis, bit):
    mask = 2**bit
    pairs = [(source, source ^ mask) for source in range(lax.axis_size(axis))]
    return lax.ppermute(value, axis, pairs)


def from_behind(block, axis, distance):
    devices = range(lax.axis_size(axis))
    route = [(i - distance, i) for i in devices if i - distance in devices]
    return lax.ppermute(block, axis, route)


def kernel_block(left_pts, right_pts):
    distance = jnp.zeros((left_pts.shape[1], right_pts.shape[1]), jnp.float32)
    for axis_id in range(3):
        offset_gap = left_pts[axis_id][:, None] - right_pts[axis_id][None, :]
        distance = distance + offset_gap * offset_gap
    return INV_FOUR_PI * lax.rsqrt(distance + DELTA_SQ)


def transposed_dot(matrix, values):
    return lax.dot_general(matrix, values, (((0,), (0,)), ((), ())), precision=HIGHEST)


def listed_sum(own_coords, entries, fetcher, width):

    def advance(running, partner):
        coords, values = fetcher(jnp.maximum(partner, 0))
        contrib = jnp.dot(kernel_block(own_coords, coords), values, precision=HIGHEST)
        return (running + jnp.where(partner >= 0, contrib, 0.0), None)

    start_value = jnp.zeros((own_coords.shape[1], width), jnp.float32)
    result, _ = lax.scan(advance, start_value, entries)
    return result


def pair_total(partial_value, levels):
    for bit_index in range(levels):
        partial_value = partial_value + from_partner(partial_value, "leaf", bit_index)
    return partial_value


def join_rows(block, levels, device):
    for bit_index in range(levels):
        other = from_partner(block, "leaf", bit_index)
        upper = device // 2**bit_index % 2
        block = jnp.where(
            upper == 0, jnp.concatenate([block, other], 0), jnp.concatenate([other, block], 0)
        )
    return block


def near_window(shipped):
    gathered = []
    for distance in range(-REACH, REACH + 1):
        if distance == 0:
            gathered.append(shipped)
        else:
            gathered.append(from_behind(shipped, "leaf", -distance))
    return jnp.stack(gathered)


def coef_window(shipped):
    gathered = []
    for distance in range(-REACH, REACH + 1):
        if distance == 0:
            gathered.append(shipped)
        else:
            gathered.append(from_behind(shipped, "leaf", -distance))
    return jnp.stack(gathered)


def partner_stack(coefs, stride):
    gathered = []
    for offset in list(range(-FAR_REACH, 0)) + list(range(1, FAR_REACH + 1)):
        gathered.append(from_behind(coefs, "leaf", -offset * stride))
    stacked = jnp.stack(gathered)

    def slot_of(distance):
        return distance + FAR_REACH - (distance > 0).astype(jnp.int32)

    return (stacked, slot_of)


def middle_level(coefs, skeletons, lists, transfer_rows, above, stride, device):
    width = coefs.shape[1]
    rank_rows = coefs.shape[0] // stride
    cluster = device // stride
    member = device % stride
    own_full = lax.dynamic_index_in_dim(skeletons, cluster, 0, keepdims=False)
    own_coords = lax.dynamic_slice_in_dim(own_full, member * rank_rows, rank_rows, 1)
    stacked, slot_of = partner_stack(coefs, stride)

    def fetcher(partner):
        coords = lax.dynamic_index_in_dim(skeletons, partner, 0, keepdims=False)
        position = jnp.clip(slot_of(partner - cluster), 0, stacked.shape[0] - 1)
        return (coords, lax.dynamic_index_in_dim(stacked, position, 0, keepdims=False))

    entries = lax.dynamic_index_in_dim(lists, cluster, 0, keepdims=False)
    rows_here = listed_sum(own_coords, entries, fetcher, width) + jnp.dot(
        transfer_rows, above, precision=HIGHEST
    )
    return join_rows(rows_here, stride.bit_length() - 1, device)


def per_device(
    vectors,
    points,
    leaf_basis,
    transfer_leaf,
    transfer_pair,
    transfer_quad,
    skel_leaf,
    skel_pair,
    skel_quad,
    skel_top,
    near_list,
    far_leaf,
    far_pair,
    far_quad,
    far_top,
):
    leaf_points = vectors.shape[1]
    width = vectors.shape[2]
    rank = leaf_basis.shape[2]
    device = lax.axis_index("leaf")
    own_points = points[0]
    shipped = jnp.concatenate(
        [vectors[0], own_points.reshape(3 * leaf_points // width, width)], axis=0
    )
    near_rim = near_window(shipped)

    def near_fetch(partner):
        position = jnp.clip(partner - device + REACH, 0, 2 * REACH)
        block = lax.dynamic_index_in_dim(near_rim, position, 0, keepdims=False)
        return (block[leaf_points:].reshape(3, leaf_points), block[:leaf_points])

    near_field = listed_sum(own_points, near_list[0], near_fetch, width)
    coef_leaf = transposed_dot(leaf_basis[0], vectors[0])
    coef_pair = pair_total(transposed_dot(transfer_leaf[0], coef_leaf), 1)
    pair_rows = lax.dynamic_slice_in_dim(coef_pair, device % 2 * (rank // 2), rank // 2, 0)
    coef_quad = pair_total(transposed_dot(transfer_pair, pair_rows), 2)
    quad_rows = lax.dynamic_slice_in_dim(coef_quad, device % 4 * (rank // 4), rank // 4, 0)
    coef_top = pair_total(transposed_dot(transfer_quad, quad_rows), 3)
    top_cluster = device // 8
    top_member = device % 8
    top_rows_own = lax.dynamic_slice_in_dim(coef_top, top_member * (rank // 8), rank // 8, 0)
    top_coords = lax.dynamic_index_in_dim(skel_top, top_cluster, 0, keepdims=False)
    top_entries = lax.dynamic_index_in_dim(far_top, top_cluster, 0, keepdims=False)
    all_top = lax.all_gather(top_rows_own, "leaf", axis=0, tiled=True).reshape(-1, rank, width)

    def top_fetch(partner):
        coords = lax.dynamic_index_in_dim(skel_top, partner, 0, keepdims=False)
        return (coords, lax.dynamic_index_in_dim(all_top, partner, 0, keepdims=False))

    local_top = listed_sum(top_coords, top_entries, top_fetch, width)
    local_quad = middle_level(coef_quad, skel_quad, far_quad, transfer_quad, local_top, 4, device)
    local_pair = middle_level(coef_pair, skel_pair, far_pair, transfer_pair, local_quad, 2, device)
    leaf_ship = jnp.concatenate([coef_leaf, skel_leaf[0]], axis=0)
    leaf_rim = coef_window(leaf_ship)

    def leaf_fetch(partner):
        position = jnp.clip(partner - device + REACH, 0, 2 * REACH)
        block = lax.dynamic_index_in_dim(leaf_rim, position, 0, keepdims=False)
        return (block[rank:], block[:rank])

    local_leaf = listed_sum(skel_leaf[0], far_leaf[0], leaf_fetch, width) + jnp.dot(
        transfer_leaf[0], local_pair, precision=HIGHEST
    )
    product = near_field + jnp.dot(leaf_basis[0], local_leaf, precision=HIGHEST)
    return product[None]


def solution(mesh):
    placed = (
        P("leaf", None, None),
        P("leaf", None, None),
        P("leaf", None, None),
        P("leaf", None, None),
        P("leaf", None),
        P("leaf", None),
        P("leaf", None, None),
        P(),
        P(),
        P(),
        P("leaf", None),
        P("leaf", None),
        P(),
        P(),
        P(),
    )
    return jax.shard_map(
        per_device, mesh=mesh, in_specs=placed, out_specs=P("leaf", None, None), check_vma=False
    )
```

profile of v0, /device:TPU:1, one launch (start us, length us, event | category | flops | bytes accessed | tf_op | source)
XLA Modules:
  0.0 703.7 jit_solution(9183280712991490266)
XLA Ops:
  9.1 9.6 %collective-permute-start.16 = (f32[131,128]{1,0:T(8,128)S(1)}, f32[131,128]{1,0:T(8,128)S(1)}, u32[]{:S(2)}, u32[]{:S(2)}) collective-permute-start(f32[131,128]{1,0:T(8,128)S(1)} %pad_maximum_fusion.1), channel_id=1, source_target_pairs={{0,8},{1,9},{2,10},{3,11},{4,12},{5,13},{6,14},{7,15},{8,16},{9,17... | collective-permute-start | bytes 201224 | tf_op jit(solution)/shard_map/ppermute | solution.py:22
  18.7 9.7 %collective-permute-start.17 = (f32[131,128]{1,0:T(8,128)S(1)}, f32[131,128]{1,0:T(8,128)S(1)}, u32[]{:S(2)}, u32[]{:S(2)}) collective-permute-start(f32[131,128]{1,0:T(8,128)S(1)} %pad_maximum_fusion.1), channel_id=1, source_target_pairs={{0,7},{1,8},{2,9},{3,10},{4,11},{5,12},{6,13},{7,14},{8,15},{9,16}... | collective-permute-start | bytes 201224 | tf_op jit(solution)/shard_map/ppermute | solution.py:22
  71.0 10.2 %collective-permute-start = (f32[524,128]{1,0:T(8,128)S(1)}, f32[524,128]{1,0:T(8,128)S(1)}, u32[]{:S(2)}, u32[]{:S(2)}) collective-permute-start(f32[524,128]{1,0:T(8,128)S(1)} %pad_maximum_fusion), channel_id=1, source_target_pairs={{0,8},{1,9},{2,10},{3,11},{4,12},{5,13},{6,14},{7,15},{8,16},{9,17... | collective-permute-start | bytes 804872 | tf_op jit(solution)/shard_map/ppermute | solution.py:22
  81.3 8.1 %collective-permute-start.1 = (f32[524,128]{1,0:T(8,128)S(1)}, f32[524,128]{1,0:T(8,128)S(1)}, u32[]{:S(2)}, u32[]{:S(2)}) collective-permute-start(f32[524,128]{1,0:T(8,128)S(1)} %pad_maximum_fusion), channel_id=1, source_target_pairs={{0,7},{1,8},{2,9},{3,10},{4,11},{5,12},{6,13},{7,14},{8,15},{9,16}... | collective-permute-start | bytes 804872 | tf_op jit(solution)/shard_map/ppermute | solution.py:22
  89.4 5.4 collective-permute-start.2
  94.9 10.9 %collective-permute-start.33 = (f32[128,128]{1,0:T(8,128)S(1)}, f32[128,128]{1,0:T(8,128)S(1)}, u32[]{:S(2)}, u32[]{:S(2)}) collective-permute-start(f32[128,128]{1,0:T(8,128)S(1)} %add.188), channel_id=1, source_target_pairs={{0,8},{1,9},{2,10},{3,11},{4,12},{5,13},{6,14},{7,15},{8,16},{9,17... | collective-permute-start | bytes 196616 | tf_op jit(solution)/shard_map/ppermute | solution.py:22
  105.8 4.1 collective-permute-start.34
  111.0 29.7 %while.56 = (s32[]{:T(128)}, f32[128,128]{1,0:T(8,128)S(1)}, s32[8]{0:T(128)S(1)}, f32[3,128]{1,0:T(4,128)S(1)}, s32[]{:T(128)}, /*index=5*/f32[17,131,128]{2,1,...) while((s32[]{:T(128)}, f32[128,128]{1,0:T(8,128)S(1)}, ...), condition=%wide.region_3.4_spmd.clone, body=%wide.region_2.3_spmd.clone.sunk | while | flops 25378828 | bytes 206616 | solution.py:45
  140.7 14.2 %collective-permute-start.35 = (f32[128,128]{1,0:T(8,128)S(1)}, f32[128,128]{1,0:T(8,128)S(1)}, u32[]{:S(2)}, u32[]{:S(2)}) collective-permute-start(f32[128,128]{1,0:T(8,128)S(1)} %add.188), channel_id=1, source_target_pairs={{0,4},{1,5},{2,6},{3,7},{4,8},{5,9},{6,10},{7,11},{8,12},{9,13},{1... | collective-permute-start | bytes 196616 | tf_op jit(solution)/shard_map/ppermute | solution.py:22
  156.3 3.7 collective-permute-done.35
  174.6 6.8 collective-permute-start.42
  184.0 23.4 %while.57 = (s32[]{:T(128)}, f32[64,128]{1,0:T(8,128)S(1)}, s32[8]{0:T(128)S(1)}, f32[3,64]{1,0:T(4,128)S(1)}, f32[256,3,128]{2,0,1:T(8,128)}, /*index=5*/s32[]{...) while((s32[]{:T(128)}, f32[64,128]{1,0:T(8,128)S(1)}, ...), condition=%wide.region_5.6_spmd.clone, body=%wide.region_4.5_spmd.clone.sunk | while | flops 12689422 | bytes 139043 | solution.py:45
  207.5 17.1 %collective-permute-start.43 = (f32[128,128]{1,0:T(8,128)S(1)}, f32[128,128]{1,0:T(8,128)S(1)}, u32[]{:S(2)}, u32[]{:S(2)}) collective-permute-start(f32[128,128]{1,0:T(8,128)S(1)} %add.194), channel_id=1, source_target_pairs={{0,16},{1,17},{2,18},{3,19},{4,20},{5,21},{6,22},{7,23},{8,24},{9,... | collective-permute-start | bytes 196616 | tf_op jit(solution)/shard_map/ppermute | solution.py:22
  224.6 14.2 %collective-permute-start.44 = (f32[128,128]{1,0:T(8,128)S(1)}, f32[128,128]{1,0:T(8,128)S(1)}, u32[]{:S(2)}, u32[]{:S(2)}) collective-permute-start(f32[128,128]{1,0:T(8,128)S(1)} %add.194), channel_id=1, source_target_pairs={{0,12},{1,13},{2,14},{3,15},{4,16},{5,17},{6,18},{7,19},{8,20},{9,... | collective-permute-start | bytes 196616 | tf_op jit(solution)/shard_map/ppermute | solution.py:22
  239.1 5.7 collective-permute-start.45
  246.2 5.5 collective-permute-done.45
  259.3 3.8 collective-permute-start.52
  265.6 7.7 %collective-permute-start.3 = (f32[524,128]{1,0:T(8,128)S(1)}, f32[524,128]{1,0:T(8,128)S(1)}, u32[]{:S(2)}, u32[]{:S(2)}) collective-permute-start(f32[524,128]{1,0:T(8,128)S(1)} %pad_maximum_fusion), channel_id=1, source_target_pairs={{0,5},{1,6},{2,7},{3,8},{4,9},{5,10},{6,11},{7,12},{8,13},{9,14},{... | collective-permute-start | bytes 804872 | tf_op jit(solution)/shard_map/ppermute | solution.py:22
  273.4 5.1 collective-permute-start.53
  282.1 14.0 %collective-permute-done.49 = f32[128,128]{1,0:T(8,128)S(1)} collective-permute-done((f32[128,128]{1,0:T(8,128)S(1)}, f32[128,128]{1,0:T(8,128)S(1)}, u32[]{:S(2)}, u32[]{:S(2)}) %collective-permute-start.49) | collective-permute-done | bytes 65568 | tf_op jit(solution)/shard_map/ppermute | solution.py:22
  297.4 18.9 %collective-permute-done.50 = f32[128,128]{1,0:T(8,128)S(1)} collective-permute-done((f32[128,128]{1,0:T(8,128)S(1)}, f32[128,128]{1,0:T(8,128)S(1)}, u32[]{:S(2)}, u32[]{:S(2)}) %collective-permute-start.50) | collective-permute-done | bytes 65568 | tf_op jit(solution)/shard_map/ppermute | solution.py:22
  316.2 6.7 collective-permute-start.4
  322.9 23.4 %while.58 = (s32[]{:T(128)}, f32[32,128]{1,0:T(8,128)S(1)}, s32[8]{0:T(128)S(1)}, f32[3,32]{1,0:T(4,128)S(1)}, f32[128,3,128]{2,0,1:T(8,128)}, /*index=5*/s32[]{...) while((s32[]{:T(128)}, f32[32,128]{1,0:T(8,128)S(1)}, ...), condition=%wide.region_7.8_spmd.clone, body=%wide.region_6.7_spmd.clone.sunk | while | flops 6344718 | bytes 105507 | solution.py:45
  346.3 7.0 collective-permute-start.5
  354.0 7.0 collective-permute-start.6
  380.6 14.4 %collective-permute-done.10 = f32[524,128]{1,0:T(8,128)S(1)} collective-permute-done((f32[524,128]{1,0:T(8,128)S(1)}, f32[524,128]{1,0:T(8,128)S(1)}, u32[]{:S(2)}, u32[]{:S(2)}) %collective-permute-start.10) | collective-permute-done | bytes 268320 | tf_op jit(solution)/shard_map/ppermute | solution.py:22
  397.0 4.4 collective-permute-done.11
  402.1 22.4 %collective-permute-done.12 = f32[524,128]{1,0:T(8,128)S(1)} collective-permute-done((f32[524,128]{1,0:T(8,128)S(1)}, f32[524,128]{1,0:T(8,128)S(1)}, u32[]{:S(2)}, u32[]{:S(2)}) %collective-permute-start.12) | collective-permute-done | bytes 268320 | tf_op jit(solution)/shard_map/ppermute | solution.py:22
  425.3 9.3 %collective-permute-done.13 = f32[524,128]{1,0:T(8,128)S(1)} collective-permute-done((f32[524,128]{1,0:T(8,128)S(1)}, f32[524,128]{1,0:T(8,128)S(1)}, u32[]{:S(2)}, u32[]{:S(2)}) %collective-permute-start.13) | collective-permute-done | bytes 268320 | tf_op jit(solution)/shard_map/ppermute | solution.py:22
  435.3 137.0 %all-gather.2.cloned.1.call-done = f32[8192,128]{1,0:T(8,128)} async-done(((f32[16,128]{1,0:T(8,128)}), f32[8192,128]{1,0:T(8,128)}) %all-gather.2.cloned.1.call-update) | async-done | bytes 4194320 | tf_op jit(solution)/shard_map/all_gather | solution.py:162
  572.3 30.4 %while.59 = (s32[]{:T(128)}, f32[128,128]{1,0:T(8,128)S(1)}, s32[8]{0:T(128)S(1)}, f32[3,128]{1,0:T(4,128)S(1)}, f32[64,3,128]{2,0,1:T(8,128)}, /*index=5*/f32[6...) while((s32[]{:T(128)}, f32[128,128]{1,0:T(8,128)S(1)}, ...), condition=%wide.region_9.10_spmd.clone, body=%wide.region_8.9_spmd.clone.sunk | while | flops 25378824 | bytes 207036 | solution.py:45
  614.2 81.0 %while.55 = (s32[]{:T(128)}, f32[512,128]{1,0:T(8,128)S(1)}, s32[16]{0:T(128)S(1)}, f32[3,512]{1,0:T(4,128)S(1)}, s32[]{:T(128)}, /*index=5*/f32[17,524,128]{2,1...) while((s32[]{:T(128)}, f32[512,128]{1,0:T(8,128)S(1)}, ...), condition=%wide.region_1.2_spmd.clone, body=%wide.region_0.1_spmd.clone.sunk | while | flops 405471232 | bytes 824088 | solution.py:45
  (387 shorter events, 242.9 us)
Async XLA Ops:
  6.5 565.8 %all-gather.2.cloned.1.call-start = ((), (), s32[]{:S(2)}) async-start(), calls=%async_computation | async-start | bytes 4202496 | tf_op jit(solution)/shard_map/all_gather | solution.py:162
  9.1 41.2 %collective-permute-start.16 = (f32[131,128]{1,0:T(8,128)S(1)}, f32[131,128]{1,0:T(8,128)S(1)}, u32[]{:S(2)}, u32[]{:S(2)}) collective-permute-start(f32[131,128]{1,0:T(8,128)S(1)} %pad_maximum_fusion.1), channel_id=1, source_target_pairs={{0,8},{1,9},{2,10},{3,11},{4,12},{5,13},{6,14},{7,15},{8,16},{9,17... | collective-permute-start | bytes 201224 | tf_op jit(solution)/shard_map/ppermute | solution.py:22
  18.7 33.8 %collective-permute-start.17 = (f32[131,128]{1,0:T(8,128)S(1)}, f32[131,128]{1,0:T(8,128)S(1)}, u32[]{:S(2)}, u32[]{:S(2)}) collective-permute-start(f32[131,128]{1,0:T(8,128)S(1)} %pad_maximum_fusion.1), channel_id=1, source_target_pairs={{0,7},{1,8},{2,9},{3,10},{4,11},{5,12},{6,13},{7,14},{8,15},{9,16}... | collective-permute-start | bytes 201224 | tf_op jit(solution)/shard_map/ppermute | solution.py:22
  28.4 26.6 %collective-permute-start.18 = (f32[131,128]{1,0:T(8,128)S(1)}, f32[131,128]{1,0:T(8,128)S(1)}, u32[]{:S(2)}, u32[]{:S(2)}) collective-permute-start(f32[131,128]{1,0:T(8,128)S(1)} %pad_maximum_fusion.1), channel_id=1, source_target_pairs={{0,6},{1,7},{2,8},{3,9},{4,10},{5,11},{6,12},{7,13},{8,14},{9,15},... | collective-permute-start | bytes 201224 | tf_op jit(solution)/shard_map/ppermute | solution.py:22
  31.9 25.3 %collective-permute-start.19 = (f32[131,128]{1,0:T(8,128)S(1)}, f32[131,128]{1,0:T(8,128)S(1)}, u32[]{:S(2)}, u32[]{:S(2)}) collective-permute-start(f32[131,128]{1,0:T(8,128)S(1)} %pad_maximum_fusion.1), channel_id=1, source_target_pairs={{0,5},{1,6},{2,7},{3,8},{4,9},{5,10},{6,11},{7,12},{8,13},{9,14},{... | collective-permute-start | bytes 201224 | tf_op jit(solution)/shard_map/ppermute | solution.py:22
  63.3 17.9 %collective-permute-start.28 = (f32[131,128]{1,0:T(8,128)S(1)}, f32[131,128]{1,0:T(8,128)S(1)}, u32[]{:S(2)}, u32[]{:S(2)}) collective-permute-start(f32[131,128]{1,0:T(8,128)S(1)} %pad_maximum_fusion.1), channel_id=1, source_target_pairs={{5,0},{6,1},{7,2},{8,3},{9,4},{10,5},{11,6},{12,7},{13,8},{14,9},{... | collective-permute-start | bytes 201224 | tf_op jit(solution)/shard_map/ppermute | solution.py:22
  64.7 24.7 %collective-permute-start.29 = (f32[131,128]{1,0:T(8,128)S(1)}, f32[131,128]{1,0:T(8,128)S(1)}, u32[]{:S(2)}, u32[]{:S(2)}) collective-permute-start(f32[131,128]{1,0:T(8,128)S(1)} %pad_maximum_fusion.1), channel_id=1, source_target_pairs={{6,0},{7,1},{8,2},{9,3},{10,4},{11,5},{12,6},{13,7},{14,8},{15,9},... | collective-permute-start | bytes 201224 | tf_op jit(solution)/shard_map/ppermute | solution.py:22
  66.0 28.9 %collective-permute-start.30 = (f32[131,128]{1,0:T(8,128)S(1)}, f32[131,128]{1,0:T(8,128)S(1)}, u32[]{:S(2)}, u32[]{:S(2)}) collective-permute-start(f32[131,128]{1,0:T(8,128)S(1)} %pad_maximum_fusion.1), channel_id=1, source_target_pairs={{7,0},{8,1},{9,2},{10,3},{11,4},{12,5},{13,6},{14,7},{15,8},{16,9}... | collective-permute-start | bytes 201224 | tf_op jit(solution)/shard_map/ppermute | solution.py:22
  68.4 37.4 %collective-permute-start.31 = (f32[131,128]{1,0:T(8,128)S(1)}, f32[131,128]{1,0:T(8,128)S(1)}, u32[]{:S(2)}, u32[]{:S(2)}) collective-permute-start(f32[131,128]{1,0:T(8,128)S(1)} %pad_maximum_fusion.1), channel_id=1, source_target_pairs={{8,0},{9,1},{10,2},{11,3},{12,4},{13,5},{14,6},{15,7},{16,8},{17,9... | collective-permute-start | bytes 201224 | tf_op jit(solution)/shard_map/ppermute | solution.py:22
  71.0 275.3 %collective-permute-start = (f32[524,128]{1,0:T(8,128)S(1)}, f32[524,128]{1,0:T(8,128)S(1)}, u32[]{:S(2)}, u32[]{:S(2)}) collective-permute-start(f32[524,128]{1,0:T(8,128)S(1)} %pad_maximum_fusion), channel_id=1, source_target_pairs={{0,8},{1,9},{2,10},{3,11},{4,12},{5,13},{6,14},{7,15},{8,16},{9,17... | collective-permute-start | bytes 804872 | tf_op jit(solution)/shard_map/ppermute | solution.py:22
  81.3 272.7 %collective-permute-start.1 = (f32[524,128]{1,0:T(8,128)S(1)}, f32[524,128]{1,0:T(8,128)S(1)}, u32[]{:S(2)}, u32[]{:S(2)}) collective-permute-start(f32[524,128]{1,0:T(8,128)S(1)} %pad_maximum_fusion), channel_id=1, source_target_pairs={{0,7},{1,8},{2,9},{3,10},{4,11},{5,12},{6,13},{7,14},{8,15},{9,16}... | collective-permute-start | bytes 804872 | tf_op jit(solution)/shard_map/ppermute | solution.py:22
  89.4 272.3 %collective-permute-start.2 = (f32[524,128]{1,0:T(8,128)S(1)}, f32[524,128]{1,0:T(8,128)S(1)}, u32[]{:S(2)}, u32[]{:S(2)}) collective-permute-start(f32[524,128]{1,0:T(8,128)S(1)} %pad_maximum_fusion), channel_id=1, source_target_pairs={{0,6},{1,7},{2,8},{3,9},{4,10},{5,11},{6,12},{7,13},{8,14},{9,15},... | collective-permute-start | bytes 804872 | tf_op jit(solution)/shard_map/ppermute | solution.py:22
  94.9 45.8 %collective-permute-start.33 = (f32[128,128]{1,0:T(8,128)S(1)}, f32[128,128]{1,0:T(8,128)S(1)}, u32[]{:S(2)}, u32[]{:S(2)}) collective-permute-start(f32[128,128]{1,0:T(8,128)S(1)} %add.188), channel_id=1, source_target_pairs={{0,8},{1,9},{2,10},{3,11},{4,12},{5,13},{6,14},{7,15},{8,16},{9,17... | collective-permute-start | bytes 196616 | tf_op jit(solution)/shard_map/ppermute | solution.py:22
  105.8 49.2 %collective-permute-start.34 = (f32[128,128]{1,0:T(8,128)S(1)}, f32[128,128]{1,0:T(8,128)S(1)}, u32[]{:S(2)}, u32[]{:S(2)}) collective-permute-start(f32[128,128]{1,0:T(8,128)S(1)} %add.188), channel_id=1, source_target_pairs={{0,6},{1,7},{2,8},{3,9},{4,10},{5,11},{6,12},{7,13},{8,14},{9,15},... | collective-permute-start | bytes 196616 | tf_op jit(solution)/shard_map/ppermute | solution.py:22
  140.7 19.3 %collective-permute-start.35 = (f32[128,128]{1,0:T(8,128)S(1)}, f32[128,128]{1,0:T(8,128)S(1)}, u32[]{:S(2)}, u32[]{:S(2)}) collective-permute-start(f32[128,128]{1,0:T(8,128)S(1)} %add.188), channel_id=1, source_target_pairs={{0,4},{1,5},{2,6},{3,7},{4,8},{5,9},{6,10},{7,11},{8,12},{9,13},{1... | collective-permute-start | bytes 196616 | tf_op jit(solution)/shard_map/ppermute | solution.py:22
  174.6 32.9 %collective-permute-start.42 = (f32[128,128]{1,0:T(8,128)S(1)}, f32[128,128]{1,0:T(8,128)S(1)}, u32[]{:S(2)}, u32[]{:S(2)}) collective-permute-start(f32[128,128]{1,0:T(8,128)S(1)} %add.193), channel_id=1, source_target_pairs={{0,2},{1,3},{2,0},{3,1},{4,6},{5,7},{6,4},{7,5},{8,10},{9,11},{10,... | collective-permute-start | bytes 196616 | tf_op jit(solution)/shard_map/ppermute | solution.py:16
  207.5 31.6 %collective-permute-start.43 = (f32[128,128]{1,0:T(8,128)S(1)}, f32[128,128]{1,0:T(8,128)S(1)}, u32[]{:S(2)}, u32[]{:S(2)}) collective-permute-start(f32[128,128]{1,0:T(8,128)S(1)} %add.194), channel_id=1, source_target_pairs={{0,16},{1,17},{2,18},{3,19},{4,20},{5,21},{6,22},{7,23},{8,24},{9,... | collective-permute-start | bytes 196616 | tf_op jit(solution)/shard_map/ppermute | solution.py:22
  224.6 20.3 %collective-permute-start.44 = (f32[128,128]{1,0:T(8,128)S(1)}, f32[128,128]{1,0:T(8,128)S(1)}, u32[]{:S(2)}, u32[]{:S(2)}) collective-permute-start(f32[128,128]{1,0:T(8,128)S(1)} %add.194), channel_id=1, source_target_pairs={{0,12},{1,13},{2,14},{3,15},{4,16},{5,17},{6,18},{7,19},{8,20},{9,... | collective-permute-start | bytes 196616 | tf_op jit(solution)/shard_map/ppermute | solution.py:22
  258.0 15.3 %collective-permute-start.48 = (f32[128,128]{1,0:T(8,128)S(1)}, f32[128,128]{1,0:T(8,128)S(1)}, u32[]{:S(2)}, u32[]{:S(2)}) collective-permute-start(f32[128,128]{1,0:T(8,128)S(1)} %add.194), channel_id=1, source_target_pairs={{8,0},{9,1},{10,2},{11,3},{12,4},{13,5},{14,6},{15,7},{16,8},{17,9... | collective-permute-start | bytes 196616 | tf_op jit(solution)/shard_map/ppermute | solution.py:22
  265.6 98.8 %collective-permute-start.3 = (f32[524,128]{1,0:T(8,128)S(1)}, f32[524,128]{1,0:T(8,128)S(1)}, u32[]{:S(2)}, u32[]{:S(2)}) collective-permute-start(f32[524,128]{1,0:T(8,128)S(1)} %pad_maximum_fusion), channel_id=1, source_target_pairs={{0,5},{1,6},{2,7},{3,8},{4,9},{5,10},{6,11},{7,12},{8,13},{9,14},{... | collective-permute-start | bytes 804872 | tf_op jit(solution)/shard_map/ppermute | solution.py:22
  280.1 15.9 %collective-permute-start.49 = (f32[128,128]{1,0:T(8,128)S(1)}, f32[128,128]{1,0:T(8,128)S(1)}, u32[]{:S(2)}, u32[]{:S(2)}) collective-permute-start(f32[128,128]{1,0:T(8,128)S(1)} %add.194), channel_id=1, source_target_pairs={{12,0},{13,1},{14,2},{15,3},{16,4},{17,5},{18,6},{19,7},{20,8},{21... | collective-permute-start | bytes 196616 | tf_op jit(solution)/shard_map/ppermute | solution.py:22
  296.1 20.2 %collective-permute-start.50 = (f32[128,128]{1,0:T(8,128)S(1)}, f32[128,128]{1,0:T(8,128)S(1)}, u32[]{:S(2)}, u32[]{:S(2)}) collective-permute-start(f32[128,128]{1,0:T(8,128)S(1)} %add.194), channel_id=1, source_target_pairs={{16,0},{17,1},{18,2},{19,3},{20,4},{21,5},{22,6},{23,7},{24,8},{25... | collective-permute-start | bytes 196616 | tf_op jit(solution)/shard_map/ppermute | solution.py:22
  316.2 51.3 %collective-permute-start.4 = (f32[524,128]{1,0:T(8,128)S(1)}, f32[524,128]{1,0:T(8,128)S(1)}, u32[]{:S(2)}, u32[]{:S(2)}) collective-permute-start(f32[524,128]{1,0:T(8,128)S(1)} %pad_maximum_fusion), channel_id=1, source_target_pairs={{0,4},{1,5},{2,6},{3,7},{4,8},{5,9},{6,10},{7,11},{8,12},{9,13},{1... | collective-permute-start | bytes 804872 | tf_op jit(solution)/shard_map/ppermute | solution.py:22
  346.3 23.2 %collective-permute-start.5 = (f32[524,128]{1,0:T(8,128)S(1)}, f32[524,128]{1,0:T(8,128)S(1)}, u32[]{:S(2)}, u32[]{:S(2)}) collective-permute-start(f32[524,128]{1,0:T(8,128)S(1)} %pad_maximum_fusion), channel_id=1, source_target_pairs={{0,3},{1,4},{2,5},{3,6},{4,7},{5,8},{6,9},{7,10},{8,11},{9,12},{10... | collective-permute-start | bytes 804872 | tf_op jit(solution)/shard_map/ppermute | solution.py:22
  354.0 17.6 %collective-permute-start.6 = (f32[524,128]{1,0:T(8,128)S(1)}, f32[524,128]{1,0:T(8,128)S(1)}, u32[]{:S(2)}, u32[]{:S(2)}) collective-permute-start(f32[524,128]{1,0:T(8,128)S(1)} %pad_maximum_fusion), channel_id=1, source_target_pairs={{0,2},{1,3},{2,4},{3,5},{4,6},{5,7},{6,8},{7,9},{8,10},{9,11},{10,... | collective-permute-start | bytes 804872 | tf_op jit(solution)/shard_map/ppermute | solution.py:22
  369.5 25.5 %collective-permute-start.10 = (f32[524,128]{1,0:T(8,128)S(1)}, f32[524,128]{1,0:T(8,128)S(1)}, u32[]{:S(2)}, u32[]{:S(2)}) collective-permute-start(f32[524,128]{1,0:T(8,128)S(1)} %pad_maximum_fusion), channel_id=1, source_target_pairs={{3,0},{4,1},{5,2},{6,3},{7,4},{8,5},{9,6},{10,7},{11,8},{12,9},{13... | collective-permute-start | bytes 804872 | tf_op jit(solution)/shard_map/ppermute | solution.py:22
  371.6 29.8 %collective-permute-start.11 = (f32[524,128]{1,0:T(8,128)S(1)}, f32[524,128]{1,0:T(8,128)S(1)}, u32[]{:S(2)}, u32[]{:S(2)}) collective-permute-start(f32[524,128]{1,0:T(8,128)S(1)} %pad_maximum_fusion), channel_id=1, source_target_pairs={{4,0},{5,1},{6,2},{7,3},{8,4},{9,5},{10,6},{11,7},{12,8},{13,9},{1... | collective-permute-start | bytes 804872 | tf_op jit(solution)/shard_map/ppermute | solution.py:22
  373.7 50.8 %collective-permute-start.12 = (f32[524,128]{1,0:T(8,128)S(1)}, f32[524,128]{1,0:T(8,128)S(1)}, u32[]{:S(2)}, u32[]{:S(2)}) collective-permute-start(f32[524,128]{1,0:T(8,128)S(1)} %pad_maximum_fusion), channel_id=1, source_target_pairs={{5,0},{6,1},{7,2},{8,3},{9,4},{10,5},{11,6},{12,7},{13,8},{14,9},{... | collective-permute-start | bytes 804872 | tf_op jit(solution)/shard_map/ppermute | solution.py:22
  376.5 58.1 %collective-permute-start.13 = (f32[524,128]{1,0:T(8,128)S(1)}, f32[524,128]{1,0:T(8,128)S(1)}, u32[]{:S(2)}, u32[]{:S(2)}) collective-permute-start(f32[524,128]{1,0:T(8,128)S(1)} %pad_maximum_fusion), channel_id=1, source_target_pairs={{6,0},{7,1},{8,2},{9,3},{10,4},{11,5},{12,6},{13,7},{14,8},{15,9},... | collective-permute-start | bytes 804872 | tf_op jit(solution)/shard_map/ppermute | solution.py:22
  378.5 226.6 %collective-permute-start.14 = (f32[524,128]{1,0:T(8,128)S(1)}, f32[524,128]{1,0:T(8,128)S(1)}, u32[]{:S(2)}, u32[]{:S(2)}) collective-permute-start(f32[524,128]{1,0:T(8,128)S(1)} %pad_maximum_fusion), channel_id=1, source_target_pairs={{7,0},{8,1},{9,2},{10,3},{11,4},{12,5},{13,6},{14,7},{15,8},{16,9}... | collective-permute-start | bytes 804872 | tf_op jit(solution)/shard_map/ppermute | solution.py:22
  395.0 214.1 %collective-permute-start.15 = (f32[524,128]{1,0:T(8,128)S(1)}, f32[524,128]{1,0:T(8,128)S(1)}, u32[]{:S(2)}, u32[]{:S(2)}) collective-permute-start(f32[524,128]{1,0:T(8,128)S(1)} %pad_maximum_fusion), channel_id=1, source_target_pairs={{8,0},{9,1},{10,2},{11,3},{12,4},{13,5},{14,6},{15,7},{16,8},{17,9... | collective-permute-start | bytes 804872 | tf_op jit(solution)/shard_map/ppermute | solution.py:22
  610.9 84.5 %collective-permute-start.56 = (f32[64,128]{1,0:T(8,128)S(1)}, f32[64,128]{1,0:T(8,128)S(1)}, u32[]{:S(2)}, u32[]{:S(2)}) collective-permute-start(f32[64,128]{1,0:T(8,128)S(1)} %add.202), channel_id=1, source_target_pairs={{0,1},{1,0},{2,3},{3,2},{4,5},{5,4},{6,7},{7,6},{8,9},{9,8},{10,11... | collective-permute-start | bytes 98312 | tf_op jit(solution)/shard_map/ppermute | solution.py:16
  (34 other events, 1276.8 us)
Sparse Core Ops, SparseCore 0:
  282.2 290.0 all-gather.1
where the time goes:
time: 710 us; the launch traced here: 704 us
  waiting for transfers between devices  249 us (35%)
  starting transfers between devices  223 us (31%)
  local copies, waits for them, and re-layouts  85.7 us (12%)
  matrix products  64.8 us (9%)
  loops' own time  63 us (9%)
  between operations  14.7 us (2%)
    ppermute x48, starting transfers between devices, from_behind(): return lax.ppermute(block, axis, route)  191 us
    all_gather x1, waiting for transfers between devices, per_device(): lax.all_gather(top_rows_own, 'leaf', axis=0, tiled=True)  137 us
    ppermute x48, waiting for transfers between devices, from_behind(): return lax.ppermute(block, axis, route)  105 us
    another operation x5, loops' own time, listed_sum(): result, _ = lax.scan(advance, start_value, entries)  63 us
    dot_general x48, matrix products, advance(): jnp.dot(kernel_block(own_coords, coords), values, precision=HIGHEST)  59.8 us
    sub x80, local copies, waits for them, and re-layouts, kernel_block(): offset_gap = left_pts[axis_id][:, None] - right_pts[axis_id][None, :]  36.6 us
    ppermute x9, starting transfers between devices, from_partner(): return lax.ppermute(value, axis, pairs)  32 us
    dynamic_slice x48, local copies, waits for them, and re-layouts, listed_sum(): result, _ = lax.scan(advance, start_value, entries)  28.5 us
  transfers between devices with their start and end apart: 58, of which 23 were waited for; matrix products, arithmetic and copies ran while one was open for 21% of the time, Pallas kernels for 0%

commit v1 on v0

--- a/solution.py
+++ b/solution.py
@@ -2,6 +2,7 @@
 import jax.numpy as jnp
 from jax import lax
 from jax.sharding import PartitionSpec as P
+from jax.lax import all_to_all, psum
 
 REACH = 8
 FAR_REACH = 4
@@ -159,7 +160,16 @@
     top_rows_own = lax.dynamic_slice_in_dim(coef_top, top_member * (rank // 8), rank // 8, 0)
     top_coords = lax.dynamic_index_in_dim(skel_top, top_cluster, 0, keepdims=False)
     top_entries = lax.dynamic_index_in_dim(far_top, top_cluster, 0, keepdims=False)
-    all_top = lax.all_gather(top_rows_own, "leaf", axis=0, tiled=True).reshape(-1, rank, width)
+    _apply_plane = lambda local_x, d0: jnp.concatenate(
+        all_to_all(
+            jnp.stack([local_x for _ in range(psum(1, "leaf"))]),
+            "leaf",
+            split_axis=0,
+            concat_axis=0,
+        ),
+        d0,
+    )
+    all_top = _apply_plane(top_rows_own, 0).reshape(-1, rank, width)
 
     def top_fetch(partner):
         coords = lax.dynamic_index_in_dim(skel_top, partner, 0, keepdims=False)

time: 710 us -> 848 us (1.19)
  the two profiles are of different devices: /device:TPU:1 before, /device:TPU:399 now
where the time goes in v1:
time: 848 us; the launch traced here: 842 us
  waiting for transfers between devices  353 us (42%)
  starting transfers between devices  269 us (32%)
  local copies, waits for them, and re-layouts  87.9 us (10%)
  matrix products  64.7 us (8%)
  loops' own time  62.8 us (7%)
    ppermute x48, waiting for transfers between devices, from_behind(): return lax.ppermute(block, axis, route)  292 us
    ppermute x48, starting transfers between devices, from_behind(): return lax.ppermute(block, axis, route)  196 us
    another operation x5, loops' own time, listed_sum(): result, _ = lax.scan(advance, start_value, entries)  62.8 us
    ppermute x9, waiting for transfers between devices, from_partner(): return lax.ppermute(value, axis, pairs)  61.1 us
    dot_general x48, matrix products, advance(): jnp.dot(kernel_block(own_coords, coords), values, precision=HIGHEST)  59.8 us
    ppermute x9, starting transfers between devices, from_partner(): return lax.ppermute(value, axis, pairs)  42.5 us
    sub x80, local copies, waits for them, and re-layouts, kernel_block(): offset_gap = left_pts[axis_id][:, None] - right_pts[axis_id][None, :]  36.5 us
    all_to_all x1, starting transfers between devices, per_device(): all_to_all(jnp.stack([local_x for _ in range(psum(1, 'leaf'))]), 'leaf',...  30.6 us
  transfers between devices with their start and end apart: 58, of which 23 were waited for; matrix products, arithmetic and copies ran while one was open for 18% of the time, Pallas kernels for 0%

profile of v1, /device:TPU:399, one launch (start us, length us, event | category | flops | bytes accessed | tf_op | source)
XLA Modules:
  0.0 842.0 jit_solution(15027906183839901300)
XLA Ops:
  4.5 5.4 collective-permute-start.17
  9.9 6.3 collective-permute-start.18
  16.1 4.9 collective-permute-start.19
  63.9 5.8 collective-permute-start.30
  69.7 6.0 collective-permute-start.31
  78.9 6.2 collective-permute-start
  87.4 29.6 %collective-permute-done.42 = f32[128,128]{1,0:T(8,128)S(1)} collective-permute-done((f32[128,128]{1,0:T(8,128)S(1)}, f32[128,128]{1,0:T(8,128)S(1)}, u32[]{:S(2)}, u32[]{:S(2)}) %collective-permute-start.42) | collective-permute-done | bytes 65568 | tf_op jit(solution)/shard_map/ppermute | solution.py:17
  128.7 14.6 %collective-permute-done.52 = f32[128,128]{1,0:T(8,128)S(1)} collective-permute-done((f32[128,128]{1,0:T(8,128)S(1)}, f32[128,128]{1,0:T(8,128)S(1)}, u32[]{:S(2)}, u32[]{:S(2)}) %collective-permute-start.52) | collective-permute-done | bytes 65568 | tf_op jit(solution)/shard_map/ppermute | solution.py:17
  143.3 14.2 %collective-permute-start.3 = (f32[524,128]{1,0:T(8,128)S(1)}, f32[524,128]{1,0:T(8,128)S(1)}, u32[]{:S(2)}, u32[]{:S(2)}) collective-permute-start(f32[524,128]{1,0:T(8,128)S(1)} %pad_maximum_fusion), channel_id=1, source_target_pairs={{0,5},{1,6},{2,7},{3,8},{4,9},{5,10},{6,11},{7,12},{8,13},{9,14},{... | collective-permute-start | bytes 804872 | tf_op jit(solution)/shard_map/ppermute | solution.py:23
  161.1 12.7 %collective-permute-done.53 = f32[128,128]{1,0:T(8,128)S(1)} collective-permute-done((f32[128,128]{1,0:T(8,128)S(1)}, f32[128,128]{1,0:T(8,128)S(1)}, u32[]{:S(2)}, u32[]{:S(2)}) %collective-permute-start.53) | collective-permute-done | bytes 65568 | tf_op jit(solution)/shard_map/ppermute | solution.py:17
  178.1 30.6 %all-to-all-start = ((f32[512,16,128]{2,1,0:T(8,128)}), f32[512,16,128]{2,1,0:T(8,128)}, u32[]{:S(2)}, u32[]{:S(2)}) async-start(f32[512,16,128]{2,1,0:T(8,128)} %stack.164), calls=%async_computation | async-start | bytes 8388608 | tf_op jit(solution)/shard_map/all_to_all | solution.py:164
  208.8 29.7 %while.56 = (s32[]{:T(128)}, f32[128,128]{1,0:T(8,128)S(1)}, s32[8]{0:T(128)S(1)}, f32[3,128]{1,0:T(4,128)S(1)}, s32[]{:T(128)}, /*index=5*/f32[17,131,128]{2,1,...) while((s32[]{:T(128)}, f32[128,128]{1,0:T(8,128)S(1)}, ...), condition=%wide.region_3.4_spmd.clone, body=%wide.region_2.3_spmd.clone.sunk | while | flops 25378828 | bytes 206616 | solution.py:46
  241.5 148.5 %collective-permute-done.34 = f32[128,128]{1,0:T(8,128)S(1)} collective-permute-done((f32[128,128]{1,0:T(8,128)S(1)}, f32[128,128]{1,0:T(8,128)S(1)}, u32[]{:S(2)}, u32[]{:S(2)}) %collective-permute-start.34) | collective-permute-done | bytes 65568 | tf_op jit(solution)/shard_map/ppermute | solution.py:23
  418.0 13.7 %collective-permute-done.39 = f32[128,128]{1,0:T(8,128)S(1)} collective-permute-done((f32[128,128]{1,0:T(8,128)S(1)}, f32[128,128]{1,0:T(8,128)S(1)}, u32[]{:S(2)}, u32[]{:S(2)}) %collective-permute-start.39) | collective-permute-done | bytes 65568 | tf_op jit(solution)/shard_map/ppermute | solution.py:23
  433.7 10.0 %collective-permute-done.40 = f32[128,128]{1,0:T(8,128)S(1)} collective-permute-done((f32[128,128]{1,0:T(8,128)S(1)}, f32[128,128]{1,0:T(8,128)S(1)}, u32[]{:S(2)}, u32[]{:S(2)}) %collective-permute-start.40) | collective-permute-done | bytes 65568 | tf_op jit(solution)/shard_map/ppermute | solution.py:23
  445.6 23.5 %while.57 = (s32[]{:T(128)}, f32[64,128]{1,0:T(8,128)S(1)}, s32[8]{0:T(128)S(1)}, f32[3,64]{1,0:T(4,128)S(1)}, f32[256,3,128]{2,0,1:T(8,128)}, /*index=5*/s32[]{...) while((s32[]{:T(128)}, f32[64,128]{1,0:T(8,128)S(1)}, ...), condition=%wide.region_5.6_spmd.clone, body=%wide.region_4.5_spmd.clone.sunk | while | flops 12689422 | bytes 139043 | solution.py:46
  469.0 6.5 collective-permute-start.44
  475.5 7.1 collective-permute-done.44
  482.7 7.8 collective-permute-start.45
  497.2 5.4 collective-permute-done.46
  515.9 8.1 collective-permute-done.48
  526.0 11.8 %collective-permute-done.49 = f32[128,128]{1,0:T(8,128)S(1)} collective-permute-done((f32[128,128]{1,0:T(8,128)S(1)}, f32[128,128]{1,0:T(8,128)S(1)}, u32[]{:S(2)}, u32[]{:S(2)}) %collective-permute-start.49) | collective-permute-done | bytes 65568 | tf_op jit(solution)/shard_map/ppermute | solution.py:23
  539.7 14.8 %collective-permute-done.50 = f32[128,128]{1,0:T(8,128)S(1)} collective-permute-done((f32[128,128]{1,0:T(8,128)S(1)}, f32[128,128]{1,0:T(8,128)S(1)}, u32[]{:S(2)}, u32[]{:S(2)}) %collective-permute-start.50) | collective-permute-done | bytes 65568 | tf_op jit(solution)/shard_map/ppermute | solution.py:23
  554.5 13.4 %collective-permute-start.4 = (f32[524,128]{1,0:T(8,128)S(1)}, f32[524,128]{1,0:T(8,128)S(1)}, u32[]{:S(2)}, u32[]{:S(2)}) collective-permute-start(f32[524,128]{1,0:T(8,128)S(1)} %pad_maximum_fusion), channel_id=1, source_target_pairs={{0,4},{1,5},{2,6},{3,7},{4,8},{5,9},{6,10},{7,11},{8,12},{9,13},{1... | collective-permute-start | bytes 804872 | tf_op jit(solution)/shard_map/ppermute | solution.py:23
  568.0 23.3 %while.58 = (s32[]{:T(128)}, f32[32,128]{1,0:T(8,128)S(1)}, s32[8]{0:T(128)S(1)}, f32[3,32]{1,0:T(4,128)S(1)}, f32[128,3,128]{2,0,1:T(8,128)}, /*index=5*/s32[]{...) while((s32[]{:T(128)}, f32[32,128]{1,0:T(8,128)S(1)}, ...), condition=%wide.region_7.8_spmd.clone, body=%wide.region_6.7_spmd.clone.sunk | while | flops 6344718 | bytes 105507 | solution.py:46
  591.3 16.4 %collective-permute-start.5 = (f32[524,128]{1,0:T(8,128)S(1)}, f32[524,128]{1,0:T(8,128)S(1)}, u32[]{:S(2)}, u32[]{:S(2)}) collective-permute-start(f32[524,128]{1,0:T(8,128)S(1)} %pad_maximum_fusion), channel_id=1, source_target_pairs={{0,3},{1,4},{2,5},{3,6},{4,7},{5,8},{6,9},{7,10},{8,11},{9,12},{10... | collective-permute-start | bytes 804872 | tf_op jit(solution)/shard_map/ppermute | solution.py:23
  608.4 6.3 collective-permute-start.6
  642.3 5.8 collective-permute-start.15
  649.5 42.8 %collective-permute-done.12 = f32[524,128]{1,0:T(8,128)S(1)} collective-permute-done((f32[524,128]{1,0:T(8,128)S(1)}, f32[524,128]{1,0:T(8,128)S(1)}, u32[]{:S(2)}, u32[]{:S(2)}) %collective-permute-start.12) | collective-permute-done | bytes 268320 | tf_op jit(solution)/shard_map/ppermute | solution.py:23
  698.5 28.6 %while.59 = (s32[]{:T(128)}, f32[128,128]{1,0:T(8,128)S(1)}, s32[8]{0:T(128)S(1)}, f32[3,128]{1,0:T(4,128)S(1)}, f32[64,3,128]{2,0,1:T(8,128)}, /*index=5*/f32[6...) while((s32[]{:T(128)}, f32[128,128]{1,0:T(8,128)S(1)}, ...), condition=%wide.region_9.10_spmd.clone, body=%wide.region_8.9_spmd.clone.sunk | while | flops 25378824 | bytes 207036 | solution.py:46
  727.3 20.4 %collective-permute-start.54 = (f32[32,128]{1,0:T(8,128)S(1)}, f32[32,128]{1,0:T(8,128)S(1)}, u32[]{:S(2)}, u32[]{:S(2)}) collective-permute-start(f32[32,128]{1,0:T(8,128)S(1)} %add.201), channel_id=1, source_target_pairs={{0,1},{1,0},{2,3},{3,2},{4,5},{5,4},{6,7},{7,6},{8,9},{9,8},{10,11... | collective-permute-start | bytes 49160 | tf_op jit(solution)/shard_map/ppermute | solution.py:17
  756.8 83.6 %while.55 = (s32[]{:T(128)}, f32[512,128]{1,0:T(8,128)S(1)}, s32[16]{0:T(128)S(1)}, f32[3,512]{1,0:T(4,128)S(1)}, s32[]{:T(128)}, /*index=5*/f32[17,524,128]{2,1...) while((s32[]{:T(128)}, f32[512,128]{1,0:T(8,128)S(1)}, ...), condition=%wide.region_1.2_spmd.clone, body=%wide.region_0.1_spmd.clone.sunk | while | flops 405471232 | bytes 824088 | solution.py:46
  (387 shorter events, 302.7 us)
Async XLA Ops:
  2.5 34.0 %collective-permute-start.16 = (f32[131,128]{1,0:T(8,128)S(1)}, f32[131,128]{1,0:T(8,128)S(1)}, u32[]{:S(2)}, u32[]{:S(2)}) collective-permute-start(f32[131,128]{1,0:T(8,128)S(1)} %pad_maximum_fusion.1), channel_id=1, source_target_pairs={{0,8},{1,9},{2,10},{3,11},{4,12},{5,13},{6,14},{7,15},{8,16},{9,17... | collective-permute-start | bytes 201224 | tf_op jit(solution)/shard_map/ppermute | solution.py:23
  4.5 35.4 %collective-permute-start.17 = (f32[131,128]{1,0:T(8,128)S(1)}, f32[131,128]{1,0:T(8,128)S(1)}, u32[]{:S(2)}, u32[]{:S(2)}) collective-permute-start(f32[131,128]{1,0:T(8,128)S(1)} %pad_maximum_fusion.1), channel_id=1, source_target_pairs={{0,7},{1,8},{2,9},{3,10},{4,11},{5,12},{6,13},{7,14},{8,15},{9,16}... | collective-permute-start | bytes 201224 | tf_op jit(solution)/shard_map/ppermute | solution.py:23
  9.9 32.7 %collective-permute-start.18 = (f32[131,128]{1,0:T(8,128)S(1)}, f32[131,128]{1,0:T(8,128)S(1)}, u32[]{:S(2)}, u32[]{:S(2)}) collective-permute-start(f32[131,128]{1,0:T(8,128)S(1)} %pad_maximum_fusion.1), channel_id=1, source_target_pairs={{0,6},{1,7},{2,8},{3,9},{4,10},{5,11},{6,12},{7,13},{8,14},{9,15},... | collective-permute-start | bytes 201224 | tf_op jit(solution)/shard_map/ppermute | solution.py:23
  16.1 29.0 %collective-permute-start.19 = (f32[131,128]{1,0:T(8,128)S(1)}, f32[131,128]{1,0:T(8,128)S(1)}, u32[]{:S(2)}, u32[]{:S(2)}) collective-permute-start(f32[131,128]{1,0:T(8,128)S(1)} %pad_maximum_fusion.1), channel_id=1, source_target_pairs={{0,5},{1,6},{2,7},{3,8},{4,9},{5,10},{6,11},{7,12},{8,13},{9,14},{... | collective-permute-start | bytes 201224 | tf_op jit(solution)/shard_map/ppermute | solution.py:23
  51.0 18.7 %collective-permute-start.26 = (f32[131,128]{1,0:T(8,128)S(1)}, f32[131,128]{1,0:T(8,128)S(1)}, u32[]{:S(2)}, u32[]{:S(2)}) collective-permute-start(f32[131,128]{1,0:T(8,128)S(1)} %pad_maximum_fusion.1), channel_id=1, source_target_pairs={{3,0},{4,1},{5,2},{6,3},{7,4},{8,5},{9,6},{10,7},{11,8},{12,9},{13... | collective-permute-start | bytes 201224 | tf_op jit(solution)/shard_map/ppermute | solution.py:23
  54.9 20.8 %collective-permute-start.27 = (f32[131,128]{1,0:T(8,128)S(1)}, f32[131,128]{1,0:T(8,128)S(1)}, u32[]{:S(2)}, u32[]{:S(2)}) collective-permute-start(f32[131,128]{1,0:T(8,128)S(1)} %pad_maximum_fusion.1), channel_id=1, source_target_pairs={{4,0},{5,1},{6,2},{7,3},{8,4},{9,5},{10,6},{11,7},{12,8},{13,9},{1... | collective-permute-start | bytes 201224 | tf_op jit(solution)/shard_map/ppermute | solution.py:23
  59.2 25.9 %collective-permute-start.28 = (f32[131,128]{1,0:T(8,128)S(1)}, f32[131,128]{1,0:T(8,128)S(1)}, u32[]{:S(2)}, u32[]{:S(2)}) collective-permute-start(f32[131,128]{1,0:T(8,128)S(1)} %pad_maximum_fusion.1), channel_id=1, source_target_pairs={{5,0},{6,1},{7,2},{8,3},{9,4},{10,5},{11,6},{12,7},{13,8},{14,9},{... | collective-permute-start | bytes 201224 | tf_op jit(solution)/shard_map/ppermute | solution.py:23
  61.9 57.4 %collective-permute-start.29 = (f32[131,128]{1,0:T(8,128)S(1)}, f32[131,128]{1,0:T(8,128)S(1)}, u32[]{:S(2)}, u32[]{:S(2)}) collective-permute-start(f32[131,128]{1,0:T(8,128)S(1)} %pad_maximum_fusion.1), channel_id=1, source_target_pairs={{6,0},{7,1},{8,2},{9,3},{10,4},{11,5},{12,6},{13,7},{14,8},{15,9},... | collective-permute-start | bytes 201224 | tf_op jit(solution)/shard_map/ppermute | solution.py:23
  63.9 60.7 %collective-permute-start.30 = (f32[131,128]{1,0:T(8,128)S(1)}, f32[131,128]{1,0:T(8,128)S(1)}, u32[]{:S(2)}, u32[]{:S(2)}) collective-permute-start(f32[131,128]{1,0:T(8,128)S(1)} %pad_maximum_fusion.1), channel_id=1, source_target_pairs={{7,0},{8,1},{9,2},{10,3},{11,4},{12,5},{13,6},{14,7},{15,8},{16,9}... | collective-permute-start | bytes 201224 | tf_op jit(solution)/shard_map/ppermute | solution.py:23
  69.7 87.8 %collective-permute-start.31 = (f32[131,128]{1,0:T(8,128)S(1)}, f32[131,128]{1,0:T(8,128)S(1)}, u32[]{:S(2)}, u32[]{:S(2)}) collective-permute-start(f32[131,128]{1,0:T(8,128)S(1)} %pad_maximum_fusion.1), channel_id=1, source_target_pairs={{8,0},{9,1},{10,2},{11,3},{12,4},{13,5},{14,6},{15,7},{16,8},{17,9... | collective-permute-start | bytes 201224 | tf_op jit(solution)/shard_map/ppermute | solution.py:23
  78.9 512.4 %collective-permute-start = (f32[524,128]{1,0:T(8,128)S(1)}, f32[524,128]{1,0:T(8,128)S(1)}, u32[]{:S(2)}, u32[]{:S(2)}) collective-permute-start(f32[524,128]{1,0:T(8,128)S(1)} %pad_maximum_fusion), channel_id=1, source_target_pairs={{0,8},{1,9},{2,10},{3,11},{4,12},{5,13},{6,14},{7,15},{8,16},{9,17... | collective-permute-start | bytes 804872 | tf_op jit(solution)/shard_map/ppermute | solution.py:23
  85.1 32.0 %collective-permute-start.42 = (f32[128,128]{1,0:T(8,128)S(1)}, f32[128,128]{1,0:T(8,128)S(1)}, u32[]{:S(2)}, u32[]{:S(2)}) collective-permute-start(f32[128,128]{1,0:T(8,128)S(1)} %add.193), channel_id=1, source_target_pairs={{0,2},{1,3},{2,0},{3,1},{4,6},{5,7},{6,4},{7,5},{8,10},{9,11},{10,... | collective-permute-start | bytes 196616 | tf_op jit(solution)/shard_map/ppermute | solution.py:17
  117.1 491.3 %collective-permute-start.1 = (f32[524,128]{1,0:T(8,128)S(1)}, f32[524,128]{1,0:T(8,128)S(1)}, u32[]{:S(2)}, u32[]{:S(2)}) collective-permute-start(f32[524,128]{1,0:T(8,128)S(1)} %pad_maximum_fusion), channel_id=1, source_target_pairs={{0,7},{1,8},{2,9},{3,10},{4,11},{5,12},{6,13},{7,14},{8,15},{9,16}... | collective-permute-start | bytes 804872 | tf_op jit(solution)/shard_map/ppermute | solution.py:23
  122.6 492.9 %collective-permute-start.2 = (f32[524,128]{1,0:T(8,128)S(1)}, f32[524,128]{1,0:T(8,128)S(1)}, u32[]{:S(2)}, u32[]{:S(2)}) collective-permute-start(f32[524,128]{1,0:T(8,128)S(1)} %pad_maximum_fusion), channel_id=1, source_target_pairs={{0,6},{1,7},{2,8},{3,9},{4,10},{5,11},{6,12},{7,13},{8,14},{9,15},... | collective-permute-start | bytes 804872 | tf_op jit(solution)/shard_map/ppermute | solution.py:23
  124.5 18.7 %collective-permute-start.52 = (f32[128,128]{1,0:T(8,128)S(1)}, f32[128,128]{1,0:T(8,128)S(1)}, u32[]{:S(2)}, u32[]{:S(2)}) collective-permute-start(f32[128,128]{1,0:T(8,128)S(1)} %add.196), channel_id=1, source_target_pairs={{0,2},{1,3},{2,0},{3,1},{4,6},{5,7},{6,4},{7,5},{8,10},{9,11},{10,... | collective-permute-start | bytes 196616 | tf_op jit(solution)/shard_map/ppermute | solution.py:17
  143.3 475.1 %collective-permute-start.3 = (f32[524,128]{1,0:T(8,128)S(1)}, f32[524,128]{1,0:T(8,128)S(1)}, u32[]{:S(2)}, u32[]{:S(2)}) collective-permute-start(f32[524,128]{1,0:T(8,128)S(1)} %pad_maximum_fusion), channel_id=1, source_target_pairs={{0,5},{1,6},{2,7},{3,8},{4,9},{5,10},{6,11},{7,12},{8,13},{9,14},{... | collective-permute-start | bytes 804872 | tf_op jit(solution)/shard_map/ppermute | solution.py:23
  173.8 64.7 %collective-permute-start.33 = (f32[128,128]{1,0:T(8,128)S(1)}, f32[128,128]{1,0:T(8,128)S(1)}, u32[]{:S(2)}, u32[]{:S(2)}) collective-permute-start(f32[128,128]{1,0:T(8,128)S(1)} %add.188), channel_id=1, source_target_pairs={{0,8},{1,9},{2,10},{3,11},{4,12},{5,13},{6,14},{7,15},{8,16},{9,17... | collective-permute-start | bytes 196616 | tf_op jit(solution)/shard_map/ppermute | solution.py:23
  178.1 520.4 %all-to-all-start = ((f32[512,16,128]{2,1,0:T(8,128)}), f32[512,16,128]{2,1,0:T(8,128)}, u32[]{:S(2)}, u32[]{:S(2)}) async-start(f32[512,16,128]{2,1,0:T(8,128)} %stack.164), calls=%async_computation | async-start | bytes 8388608 | tf_op jit(solution)/shard_map/all_to_all | solution.py:164
  238.5 151.5 %collective-permute-start.34 = (f32[128,128]{1,0:T(8,128)S(1)}, f32[128,128]{1,0:T(8,128)S(1)}, u32[]{:S(2)}, u32[]{:S(2)}) collective-permute-start(f32[128,128]{1,0:T(8,128)S(1)} %add.188), channel_id=1, source_target_pairs={{0,6},{1,7},{2,8},{3,9},{4,10},{5,11},{6,12},{7,13},{8,14},{9,15},... | collective-permute-start | bytes 196616 | tf_op jit(solution)/shard_map/ppermute | solution.py:23
  443.6 25.4 %collective-permute-start.43 = (f32[128,128]{1,0:T(8,128)S(1)}, f32[128,128]{1,0:T(8,128)S(1)}, u32[]{:S(2)}, u32[]{:S(2)}) collective-permute-start(f32[128,128]{1,0:T(8,128)S(1)} %add.194), channel_id=1, source_target_pairs={{0,16},{1,17},{2,18},{3,19},{4,20},{5,21},{6,22},{7,23},{8,24},{9,... | collective-permute-start | bytes 196616 | tf_op jit(solution)/shard_map/ppermute | solution.py:23
  554.5 66.9 %collective-permute-start.4 = (f32[524,128]{1,0:T(8,128)S(1)}, f32[524,128]{1,0:T(8,128)S(1)}, u32[]{:S(2)}, u32[]{:S(2)}) collective-permute-start(f32[524,128]{1,0:T(8,128)S(1)} %pad_maximum_fusion), channel_id=1, source_target_pairs={{0,4},{1,5},{2,6},{3,7},{4,8},{5,9},{6,10},{7,11},{8,12},{9,13},{1... | collective-permute-start | bytes 804872 | tf_op jit(solution)/shard_map/ppermute | solution.py:23
  591.3 35.3 %collective-permute-start.5 = (f32[524,128]{1,0:T(8,128)S(1)}, f32[524,128]{1,0:T(8,128)S(1)}, u32[]{:S(2)}, u32[]{:S(2)}) collective-permute-start(f32[524,128]{1,0:T(8,128)S(1)} %pad_maximum_fusion), channel_id=1, source_target_pairs={{0,3},{1,4},{2,5},{3,6},{4,7},{5,8},{6,9},{7,10},{8,11},{9,12},{10... | collective-permute-start | bytes 804872 | tf_op jit(solution)/shard_map/ppermute | solution.py:23
  608.4 22.4 %collective-permute-start.6 = (f32[524,128]{1,0:T(8,128)S(1)}, f32[524,128]{1,0:T(8,128)S(1)}, u32[]{:S(2)}, u32[]{:S(2)}) collective-permute-start(f32[524,128]{1,0:T(8,128)S(1)} %pad_maximum_fusion), channel_id=1, source_target_pairs={{0,2},{1,3},{2,4},{3,5},{4,6},{5,7},{6,8},{7,9},{8,10},{9,11},{10,... | collective-permute-start | bytes 804872 | tf_op jit(solution)/shard_map/ppermute | solution.py:23
  615.5 18.1 %collective-permute-start.7 = (f32[524,128]{1,0:T(8,128)S(1)}, f32[524,128]{1,0:T(8,128)S(1)}, u32[]{:S(2)}, u32[]{:S(2)}) collective-permute-start(f32[524,128]{1,0:T(8,128)S(1)} %pad_maximum_fusion), channel_id=1, source_target_pairs={{0,1},{1,2},{2,3},{3,4},{4,5},{5,6},{6,7},{7,8},{8,9},{9,10},{10,1... | collective-permute-start | bytes 804872 | tf_op jit(solution)/shard_map/ppermute | solution.py:23
  618.4 18.6 %collective-permute-start.8 = (f32[524,128]{1,0:T(8,128)S(1)}, f32[524,128]{1,0:T(8,128)S(1)}, u32[]{:S(2)}, u32[]{:S(2)}) collective-permute-start(f32[524,128]{1,0:T(8,128)S(1)} %pad_maximum_fusion), channel_id=1, source_target_pairs={{1,0},{2,1},{3,2},{4,3},{5,4},{6,5},{7,6},{8,7},{9,8},{10,9},{11,1... | collective-permute-start | bytes 804872 | tf_op jit(solution)/shard_map/ppermute | solution.py:23
  621.4 18.2 %collective-permute-start.9 = (f32[524,128]{1,0:T(8,128)S(1)}, f32[524,128]{1,0:T(8,128)S(1)}, u32[]{:S(2)}, u32[]{:S(2)}) collective-permute-start(f32[524,128]{1,0:T(8,128)S(1)} %pad_maximum_fusion), channel_id=1, source_target_pairs={{2,0},{3,1},{4,2},{5,3},{6,4},{7,5},{8,6},{9,7},{10,8},{11,9},{12,... | collective-permute-start | bytes 804872 | tf_op jit(solution)/shard_map/ppermute | solution.py:23
  633.6 58.7 %collective-permute-start.12 = (f32[524,128]{1,0:T(8,128)S(1)}, f32[524,128]{1,0:T(8,128)S(1)}, u32[]{:S(2)}, u32[]{:S(2)}) collective-permute-start(f32[524,128]{1,0:T(8,128)S(1)} %pad_maximum_fusion), channel_id=1, source_target_pairs={{5,0},{6,1},{7,2},{8,3},{9,4},{10,5},{11,6},{12,7},{13,8},{14,9},{... | collective-permute-start | bytes 804872 | tf_op jit(solution)/shard_map/ppermute | solution.py:23
  636.9 60.8 %collective-permute-start.13 = (f32[524,128]{1,0:T(8,128)S(1)}, f32[524,128]{1,0:T(8,128)S(1)}, u32[]{:S(2)}, u32[]{:S(2)}) collective-permute-start(f32[524,128]{1,0:T(8,128)S(1)} %pad_maximum_fusion), channel_id=1, source_target_pairs={{6,0},{7,1},{8,2},{9,3},{10,4},{11,5},{12,6},{13,7},{14,8},{15,9},... | collective-permute-start | bytes 804872 | tf_op jit(solution)/shard_map/ppermute | solution.py:23
  639.6 108.1 %collective-permute-start.14 = (f32[524,128]{1,0:T(8,128)S(1)}, f32[524,128]{1,0:T(8,128)S(1)}, u32[]{:S(2)}, u32[]{:S(2)}) collective-permute-start(f32[524,128]{1,0:T(8,128)S(1)} %pad_maximum_fusion), channel_id=1, source_target_pairs={{7,0},{8,1},{9,2},{10,3},{11,4},{12,5},{13,6},{14,7},{15,8},{16,9}... | collective-permute-start | bytes 804872 | tf_op jit(solution)/shard_map/ppermute | solution.py:23
  642.3 108.2 %collective-permute-start.15 = (f32[524,128]{1,0:T(8,128)S(1)}, f32[524,128]{1,0:T(8,128)S(1)}, u32[]{:S(2)}, u32[]{:S(2)}) collective-permute-start(f32[524,128]{1,0:T(8,128)S(1)} %pad_maximum_fusion), channel_id=1, source_target_pairs={{8,0},{9,1},{10,2},{11,3},{12,4},{13,5},{14,6},{15,7},{16,8},{17,9... | collective-permute-start | bytes 804872 | tf_op jit(solution)/shard_map/ppermute | solution.py:23
  727.3 21.2 %collective-permute-start.54 = (f32[32,128]{1,0:T(8,128)S(1)}, f32[32,128]{1,0:T(8,128)S(1)}, u32[]{:S(2)}, u32[]{:S(2)}) collective-permute-start(f32[32,128]{1,0:T(8,128)S(1)} %add.201), channel_id=1, source_target_pairs={{0,1},{1,0},{2,3},{3,2},{4,5},{5,4},{6,7},{7,6},{8,9},{9,8},{10,11... | collective-permute-start | bytes 49160 | tf_op jit(solution)/shard_map/ppermute | solution.py:17
  753.4 87.2 %collective-permute-start.56 = (f32[64,128]{1,0:T(8,128)S(1)}, f32[64,128]{1,0:T(8,128)S(1)}, u32[]{:S(2)}, u32[]{:S(2)}) collective-permute-start(f32[64,128]{1,0:T(8,128)S(1)} %add.202), channel_id=1, source_target_pairs={{0,1},{1,0},{2,3},{3,2},{4,5},{5,4},{6,7},{7,6},{8,9},{9,8},{10,11... | collective-permute-start | bytes 98312 | tf_op jit(solution)/shard_map/ppermute | solution.py:17
  (34 other events, 1002.8 us)
